TPU v7x, 32 devices: a whole 2x2x4 slice. The times are simulated.
32 devices in a mesh: depth: 8 (over y, x, core), tile: 4 (over z).
Axes of the slice: x: 2, y: 2, z: 4, core: 2. Of those that a mesh axis runs over, the one named last changes fastest.
Arguments:
- measured: float32 [32, 1024, 1024], P('depth', 'tile'), may hold values from 0.1 to 3
- estimate: float32 [32, 1024, 1024], P('depth', 'tile'), may hold values from 0.5 to 2
- extinction: float32 [32, 1024, 1024], P('depth', 'tile'), may hold values from 0.002 to 0.05
- psf_rows: float32 [16, 65], replicated, may hold values from 0.05 to 1
- psf_cols: float32 [16, 65], replicated, may hold values from 0.05 to 1
- stratum: int32 [32], P('depth'), may hold values from 0 to 15
- seam_flags: int32 [3], replicated, may hold values 0 or 1
Outputs:
- updated: float32 [32, 1024, 1024], P('depth', 'tile')
- projection: float32 [1024, 1024], P('tile')
All inputs are finite; a program needn't handle non-finite values.
Results may differ from a plain program's by a relative error of at most 0.000073.
Values sent between devices are 32-bit elements; how exact they have to be, the bound alone decides.
A program may use at most 128 MiB of HBM per device.

v0:
```python
import jax
import jax.numpy as jnp
from jax import lax
from jax.sharding import PartitionSpec as P


def carried_in(part, axis, combine, identity):
    place = lax.axis_index(axis)
    gathered = lax.all_gather(part, axis)
    state = jnp.zeros_like(part) + jnp.asarray(identity, part.dtype)

    def one(hop, state):
        return combine(state, lax.dynamic_index_in_dim(gathered, hop, 0, False))

    return lax.fori_loop(0, place, one, state)


def with_halo(cells, sides, width):
    for axis, dim in sides:
        count = lax.axis_size(axis)
        ends = count - 1
        head = lax.slice_in_dim(cells, 0, width, axis=dim)
        tail = lax.slice_in_dim(cells, cells.shape[dim] - width, cells.shape[dim], axis=dim)
        cells = jnp.concatenate(
            [
                lax.ppermute(tail, axis, [(i, (i + 1) % count) for i in range(ends)]),
                cells,
                lax.ppermute(head, axis, [((i + 1) % count, i) for i in range(ends)]),
            ],
            axis=dim,
        )
    return cells


def band_matrix(kernel, offsets):
    length = kernel.shape[0]
    result = jnp.zeros(offsets.shape, jnp.float32)
    for index in range(length):
        result = jnp.where(offsets == index, kernel[index], result)
    return result


def banded(kernel, row_count, col_count):
    offsets = (
        jnp.arange(col_count, dtype=jnp.int32)[None, :]
        - jnp.arange(row_count, dtype=jnp.int32)[:, None]
    )
    return band_matrix(kernel, offsets)


def lateral_apply(data, kernel, half_width):
    row_total, col_total = data.shape
    block_width = min(128, col_total)
    block_count = col_total // block_width
    padded = jnp.pad(data, ((0, 0), (block_width, block_width)))
    blocks = padded.reshape(row_total, block_count + 2, block_width)
    windows = jnp.concatenate(
        [blocks[:, :block_count], blocks[:, 1 : block_count + 1], blocks[:, 2:]], axis=2
    )
    sources = jnp.arange(3 * block_width, dtype=jnp.int32)[:, None]
    targets = jnp.arange(block_width, dtype=jnp.int32)[None, :]
    offsets = sources - targets - block_width + half_width
    matrix = band_matrix(kernel, offsets)
    result_blocks = jnp.einsum("rnk,kc->rnc", windows, matrix, precision=lax.Precision.HIGHEST)
    return result_blocks.reshape(row_total, col_total)


def combine(earlier, later):
    return earlier + later


def on_device(measured, estimate, extinction, psf_rows, psf_cols, stratum, seam_flags):
    planes, row_count, col_count = measured.shape
    half_width = (psf_rows.shape[1] - 1) // 2
    highest = lax.Precision.HIGHEST
    running = jnp.zeros(extinction.shape[1:], jnp.float32)
    prefixes = []
    for plane in range(planes):
        prefixes.append(running)
        running = running + extinction[plane]
    above = carried_in(running, "depth", combine, jnp.zeros_like(running))
    optical = above[None] + jnp.stack(prefixes)
    weighted = jnp.exp(-optical) * estimate
    strata = psf_rows.shape[0]
    picker = (stratum[:, None] == jnp.arange(strata, dtype=jnp.int32)[None, :]).astype(jnp.float32)
    vertical = jnp.dot(
        picker, psf_rows / jnp.sum(psf_rows, axis=1, keepdims=True), precision=highest
    )
    lateral = jnp.dot(
        picker, psf_cols / jnp.sum(psf_cols, axis=1, keepdims=True), precision=highest
    )
    padded = jnp.concatenate(
        [jnp.zeros((1,), jnp.float32), seam_flags.astype(jnp.float32), jnp.zeros((1,), jnp.float32)]
    )
    flags = lax.dynamic_slice_in_dim(padded, lax.axis_index("tile"), 2)

    def rim_scale(width):
        column = jnp.concatenate(
            [
                flags[0] * jnp.ones((width,), jnp.float32),
                jnp.ones((row_count,), jnp.float32),
                flags[1] * jnp.ones((width,), jnp.float32),
            ]
        )
        return column[None, :, None]

    quotients = []
    extended = with_halo(weighted, (("tile", 1),), half_width) * rim_scale(half_width)
    for plane in range(planes):
        band_rows = banded(vertical[plane], row_count, row_count + 2 * half_width)
        mixed = jnp.dot(band_rows, extended[plane], precision=highest)
        blurred = lateral_apply(mixed, lateral[plane], half_width)
        quotients.append(measured[plane] / blurred)
    quotient = with_halo(jnp.stack(quotients), (("tile", 1),), half_width) * rim_scale(half_width)
    results = []
    for plane in range(planes):
        band_back = banded(vertical[plane][::-1], row_count, row_count + 2 * half_width)
        mixed = jnp.dot(band_back, quotient[plane], precision=highest)
        spread = lateral_apply(mixed, lateral[plane][::-1], half_width)
        results.append(estimate[plane] * spread)
    updated = jnp.stack(results)
    projection = lax.pmax(jnp.max(updated, axis=0), "depth")
    return (updated, projection)


def solution(mesh):
    return jax.shard_map(
        on_device,
        mesh=mesh,
        in_specs=(
            P("depth", "tile", None),
            P("depth", "tile", None),
            P("depth", "tile", None),
            P(),
            P(),
            P("depth"),
            P(),
        ),
        out_specs=(P("depth", "tile", None), P("tile", None)),
        check_vma=False,
    )
```

profile of v0, /device:TPU:0, one launch (start us, length us, event | category | flops | bytes accessed | tf_op | source)
XLA Modules:
  0.0 986.2 jit_solution(394362127496866134)
XLA Ops:
  30.4 38.1 %all-gather.2.cloned.1.call-done = f32[8,256,1024]{2,1,0:T(8,128)} async-done(((f32[1,256,1024]{2,1,0:T(8,128)}), f32[8,256,1024]{2,1,0:T(8,128)}) %all-gather.2.cloned.1.call-update) | async-done | bytes 8388624 | tf_op jit(solution)/shard_map/all_gather | solution.py:9
  73.6 4.8 collective-permute-start
  82.6 5.6 collective-permute-done.1
  91.0 44.5 %fusion.58 = f32[256,1024]{0,1:T(8,128)S(1)} fusion(f32[4,320,1024]{2,1,0:T(8,128)S(1)} %maximum_multiply_fusion, f32[]{:T(128)} %bitcast.65, f32[]{:T(128)} %bitcast.64, f32[]{:T(128)} %bitcast.63, f32[]{:T(128)} %bitcast.62, f32[]{:T(128)} %bitcast.61, f32[]{:T(128)} %bitcast.60, f32[]{:T(128)} %bitcast.59, f32[]{:T(128)} %bitcast.58, f32[]{:T(128)} %bitcast.57, ...), kind=kOutput, calls=%fused_computation.71 | convolution fusion | flops 1017364480 | bytes 2359556
  138.9 46.7 %fusion.3 = f32[256,8,128]{0,2,1:T(8,128)} fusion(f32[256,8,128]{2,0,1:T(8,128)S(1)} %copy-done.10, f32[256,8,128]{2,0,1:T(8,128)} %copy.122, f32[256,8,128]{2,0,1:T(8,128)S(1)} %copy.121, f32[]{:T(128)} %bitcast.134, f32[]{:T(128)} %bitcast.133, f32[]{:T(128)} %bitcast.132, f32[]{:T(128)} %bitcast.131, f32[]{:T(128)} %bitcast.130, f32[]{:T(128)} %bitcast.129, ...), kind=kOutput, calls=%fused_computation.8 | convolution fusion | flops 1216020480 | bytes 4194564 | tf_op jit(solution)/shard_map/rnk,kc->rnc/dot_general | solution.py:64
  187.2 44.3 %fusion.57 = f32[256,1024]{0,1:T(8,128)S(1)} fusion(f32[4,320,1024]{2,1,0:T(8,128)} %copy-done, f32[]{:T(128)} %bitcast.201, f32[]{:T(128)} %bitcast.200, f32[]{:T(128)} %bitcast.199, f32[]{:T(128)} %bitcast.198, f32[]{:T(128)} %bitcast.197, f32[]{:T(128)} %bitcast.196, f32[]{:T(128)} %bitcast.195, f32[]{:T(128)} %bitcast.194, f32[]{:T(128)} %bitcast.193, ...), kind=kOutput, calls=%fused_computation.69 | convolution fusion | flops 1017364480 | bytes 2392576
  237.2 46.1 %fusion.9 = f32[256,8,128]{0,2,1:T(8,128)} fusion(f32[256,8,128]{2,0,1:T(8,128)} %copy.126, f32[256,8,128]{2,0,1:T(8,128)} %copy.125, f32[256,8,128]{2,0,1:T(8,128)S(1)} %copy.124, f32[]{:T(128)} %bitcast.268, f32[]{:T(128)} %bitcast.267, f32[]{:T(128)} %bitcast.266, f32[]{:T(128)} %bitcast.265, f32[]{:T(128)} %bitcast.264, f32[]{:T(128)} %bitcast.263, ...), kind=kOutput, calls=%fused_computation.14 | convolution fusion | flops 1216020480 | bytes 4194564 | tf_op jit(solution)/shard_map/rnk,kc->rnc/dot_general | solution.py:64
  284.8 45.2 %fusion.55 = f32[256,1024]{0,1:T(8,128)S(1)} fusion(f32[4,320,1024]{2,1,0:T(8,128)} %copy-done, f32[]{:T(128)} %bitcast.469, f32[]{:T(128)} %bitcast.468, f32[]{:T(128)} %bitcast.467, f32[]{:T(128)} %bitcast.466, f32[]{:T(128)} %bitcast.465, f32[]{:T(128)} %bitcast.464, f32[]{:T(128)} %bitcast.463, f32[]{:T(128)} %bitcast.462, f32[]{:T(128)} %bitcast.461, ...), kind=kOutput, calls=%fused_computation.65 | convolution fusion | flops 1017364480 | bytes 2392576
  338.2 47.1 %fusion.21 = f32[256,8,128]{0,2,1:T(8,128)} fusion(f32[256,8,128]{2,0,1:T(8,128)} %copy.132, f32[256,8,128]{2,0,1:T(8,128)} %copy.131, f32[256,8,128]{2,0,1:T(8,128)} %copy.130, f32[]{:T(128)} %bitcast.536, f32[]{:T(128)} %bitcast.535, f32[]{:T(128)} %bitcast.534, f32[]{:T(128)} %bitcast.533, f32[]{:T(128)} %bitcast.532, f32[]{:T(128)} %bitcast.531, ...), kind=kOutput, calls=%fused_computation.26 | convolution fusion | flops 1216020480 | bytes 4194564 | tf_op jit(solution)/shard_map/rnk,kc->rnc/dot_general | solution.py:64
  386.9 44.6 %fusion.56 = f32[256,1024]{0,1:T(8,128)S(1)} fusion(f32[4,320,1024]{2,1,0:T(8,128)} %copy-done, f32[]{:T(128)} %bitcast.335, f32[]{:T(128)} %bitcast.334, f32[]{:T(128)} %bitcast.333, f32[]{:T(128)} %bitcast.332, f32[]{:T(128)} %bitcast.331, f32[]{:T(128)} %bitcast.330, f32[]{:T(128)} %bitcast.329, f32[]{:T(128)} %bitcast.328, f32[]{:T(128)} %bitcast.327, ...), kind=kOutput, calls=%fused_computation.67 | convolution fusion | flops 1017364480 | bytes 2392576
  441.1 47.5 %fusion.15 = f32[256,8,128]{0,2,1:T(8,128)} fusion(f32[256,8,128]{2,0,1:T(8,128)} %copy.129, f32[256,8,128]{2,0,1:T(8,128)} %copy.128, f32[256,8,128]{2,0,1:T(8,128)} %copy.127, f32[]{:T(128)} %bitcast.402, f32[]{:T(128)} %bitcast.401, f32[]{:T(128)} %bitcast.400, f32[]{:T(128)} %bitcast.399, f32[]{:T(128)} %bitcast.398, f32[]{:T(128)} %bitcast.397, ...), kind=kOutput, calls=%fused_computation.20 | convolution fusion | flops 1216020480 | bytes 4194564 | tf_op jit(solution)/shard_map/rnk,kc->rnc/dot_general | solution.py:64
  495.9 5.1 collective-permute-start.2
  500.9 10.5 %collective-permute-done.3 = f32[4,32,1024]{2,1,0:T(8,128)S(1)} collective-permute-done((f32[4,32,1024]{2,1,0:T(8,128)S(1)}, f32[4,32,1024]{2,1,0:T(8,128)S(1)}, u32[]{:S(2)}, u32[]{:S(2)}) %collective-permute-start.3) | collective-permute-done | bytes 524320 | tf_op jit(solution)/shard_map/ppermute | solution.py:28
  514.4 44.5 %fusion.54 = f32[256,1024]{0,1:T(8,128)S(1)} fusion(f32[4,320,1024]{2,1,0:T(8,128)S(1)} %maximum_multiply_fusion.1, f32[]{:T(128)} %bitcast.65, f32[]{:T(128)} %bitcast.64, f32[]{:T(128)} %bitcast.63, f32[]{:T(128)} %bitcast.62, f32[]{:T(128)} %bitcast.61, f32[]{:T(128)} %bitcast.60, f32[]{:T(128)} %bitcast.59, f32[]{:T(128)} %bitcast.58, f32[]{:T(128)} %bitcast.57, ...), kind=kOutput, calls=%fused_computation.63 | convolution fusion | flops 1017364480 | bytes 2359556
  558.9 43.8 %fusion.53 = f32[256,1024]{0,1:T(8,128)} fusion(f32[4,320,1024]{2,1,0:T(8,128)S(1)} %maximum_multiply_fusion.1, f32[]{:T(128)} %bitcast.201, f32[]{:T(128)} %bitcast.200, f32[]{:T(128)} %bitcast.199, f32[]{:T(128)} %bitcast.198, f32[]{:T(128)} %bitcast.197, f32[]{:T(128)} %bitcast.196, f32[]{:T(128)} %bitcast.195, f32[]{:T(128)} %bitcast.194, ...), kind=kOutput, calls=%fused_computation.61 | convolution fusion | flops 1017364480 | bytes 2359556
  602.7 44.3 %fusion.52 = f32[256,1024]{0,1:T(8,128)} fusion(f32[4,320,1024]{2,1,0:T(8,128)S(1)} %maximum_multiply_fusion.1, f32[]{:T(128)} %bitcast.335, f32[]{:T(128)} %bitcast.334, f32[]{:T(128)} %bitcast.333, f32[]{:T(128)} %bitcast.332, f32[]{:T(128)} %bitcast.331, f32[]{:T(128)} %bitcast.330, f32[]{:T(128)} %bitcast.329, f32[]{:T(128)} %bitcast.328, ...), kind=kOutput, calls=%fused_computation.59 | convolution fusion | flops 1017364480 | bytes 2359556
  647.0 45.2 %fusion.51 = f32[256,1024]{0,1:T(8,128)} fusion(f32[4,320,1024]{2,1,0:T(8,128)S(1)} %maximum_multiply_fusion.1, f32[]{:T(128)} %bitcast.469, f32[]{:T(128)} %bitcast.468, f32[]{:T(128)} %bitcast.467, f32[]{:T(128)} %bitcast.466, f32[]{:T(128)} %bitcast.465, f32[]{:T(128)} %bitcast.464, f32[]{:T(128)} %bitcast.463, f32[]{:T(128)} %bitcast.462, ...), kind=kOutput, calls=%fused_computation.57 | convolution fusion | flops 1017364480 | bytes 2359556
  695.6 46.8 %fusion.27 = f32[256,8,128]{0,2,1:T(8,128)} fusion(f32[256,8,128]{2,0,1:T(8,128)S(1)} %copy-done.7, f32[256,8,128]{2,0,1:T(8,128)} %copy.134, f32[256,8,128]{2,0,1:T(8,128)S(1)} %copy.133, f32[]{:T(128)} %bitcast.134, f32[]{:T(128)} %bitcast.133, f32[]{:T(128)} %bitcast.132, f32[]{:T(128)} %bitcast.131, f32[]{:T(128)} %bitcast.130, f32[]{:T(128)} %bitcast.129, ...), kind=kOutput, calls=%fused_computation.32 | convolution fusion | flops 1216020480 | bytes 4194564 | tf_op jit(solution)/shard_map/rnk,kc->rnc/dot_general | solution.py:64
  748.4 45.9 %fusion.33 = f32[256,8,128]{0,2,1:T(8,128)} fusion(f32[256,8,128]{2,0,1:T(8,128)S(1)} %copy-done.8, f32[256,8,128]{2,0,1:T(8,128)} %copy.137, f32[256,8,128]{2,0,1:T(8,128)S(1)} %copy.136, f32[]{:T(128)} %bitcast.268, f32[]{:T(128)} %bitcast.267, f32[]{:T(128)} %bitcast.266, f32[]{:T(128)} %bitcast.265, f32[]{:T(128)} %bitcast.264, f32[]{:T(128)} %bitcast.263, ...), kind=kOutput, calls=%fused_computation.38 | convolution fusion | flops 1216020480 | bytes 4194564 | tf_op jit(solution)/shard_map/rnk,kc->rnc/dot_general | solution.py:64
  800.2 47.2 %fusion.39 = f32[256,8,128]{0,2,1:T(8,128)} fusion(f32[256,8,128]{2,0,1:T(8,128)S(1)} %copy-done.9, f32[256,8,128]{2,0,1:T(8,128)} %copy.140, f32[256,8,128]{2,0,1:T(8,128)S(1)} %copy.139, f32[]{:T(128)} %bitcast.402, f32[]{:T(128)} %bitcast.401, f32[]{:T(128)} %bitcast.400, f32[]{:T(128)} %bitcast.399, f32[]{:T(128)} %bitcast.398, f32[]{:T(128)} %bitcast.397, ...), kind=kOutput, calls=%fused_computation.44 | convolution fusion | flops 1216020480 | bytes 4194564 | tf_op jit(solution)/shard_map/rnk,kc->rnc/dot_general | solution.py:64
  854.4 47.0 %fusion.45 = f32[256,8,128]{0,2,1:T(8,128)} fusion(f32[256,8,128]{2,0,1:T(8,128)} %copy.144, f32[256,8,128]{2,0,1:T(8,128)} %copy.143, f32[256,8,128]{2,0,1:T(8,128)} %copy.142, f32[]{:T(128)} %bitcast.536, f32[]{:T(128)} %bitcast.535, f32[]{:T(128)} %bitcast.534, f32[]{:T(128)} %bitcast.533, f32[]{:T(128)} %bitcast.532, f32[]{:T(128)} %bitcast.531, ...), kind=kOutput, calls=%fused_computation.50 | convolution fusion | flops 1216020480 | bytes 4194564 | tf_op jit(solution)/shard_map/rnk,kc->rnc/dot_general | solution.py:64
  903.9 5.3 maximum_bitcast_fusion
  909.2 4.8 pad_maximum_fusion
  914.0 62.6 %all-reduce.10.cloned.1.call-done = f32[256,1024]{1,0:T(8,128)} async-done(((f32[256,1024]{1,0:T(8,128)}), f32[256,1024]{1,0:T(8,128)}) %all-reduce.10.cloned.1.call-update) | async-done | bytes 1048592 | tf_op jit(solution)/shard_map/pmax | solution.py:122
  (137 shorter events, 103.8 us)
Async XLA Ops:
  7.2 4.2 copy-start.13
  7.2 4.3 copy-start.11
  7.2 4.4 copy-start.12
  7.2 5.3 copy-start.14
  7.2 61.3 %all-gather.2.cloned.1.call-start = ((), (), s32[]{:S(2)}) async-start(), calls=%async_computation | async-start | bytes 9437184 | tf_op jit(solution)/shard_map/all_gather | solution.py:9
  11.4 965.2 %all-reduce.10.cloned.1.call-start = ((), (), s32[]{:S(2)}) async-start(), calls=%async_computation.1 | async-start | bytes 2097152 | tf_op jit(solution)/shard_map/pmax | solution.py:122
  72.3 15.9 %collective-permute-start.1 = (f32[4,32,1024]{2,1,0:T(8,128)S(1)}, f32[4,32,1024]{2,1,0:T(8,128)S(1)}, u32[]{:S(2)}, u32[]{:S(2)}) collective-permute-start(f32[4,32,1024]{2,1,0:T(8,128)S(1)} %get-tuple-element.49), channel_id=1, source_target_pairs={{1,0},{2,1},{3,2},{5,4},{6,5},{7,6},{9,8},{10,9},{11,10},{13,12},{... | collective-permute-start | bytes 1572872 | tf_op jit(solution)/shard_map/ppermute | solution.py:28
  73.6 16.3 %collective-permute-start = (f32[4,32,1024]{2,1,0:T(8,128)S(1)}, f32[4,32,1024]{2,1,0:T(8,128)S(1)}, u32[]{:S(2)}, u32[]{:S(2)}) collective-permute-start(f32[4,32,1024]{2,1,0:T(8,128)S(1)} %get-tuple-element.48), channel_id=1, source_target_pairs={{0,1},{1,2},{2,3},{4,5},{5,6},{6,7},{8,9},{9,10},{10,11},{12,13},{... | collective-permute-start | bytes 1572872 | tf_op jit(solution)/shard_map/ppermute | solution.py:26
  91.0 44.5 %copy-start = (f32[4,320,1024]{2,1,0:T(8,128)}, f32[4,320,1024]{2,1,0:T(8,128)S(1)}, u32[]{:S(2)}) copy-start(f32[4,320,1024]{2,1,0:T(8,128)S(1)} %maximum_multiply_fusion) | copy-start | bytes 15728644
  137.3 1.6 copy-start.10
  494.6 16.8 %collective-permute-start.3 = (f32[4,32,1024]{2,1,0:T(8,128)S(1)}, f32[4,32,1024]{2,1,0:T(8,128)S(1)}, u32[]{:S(2)}, u32[]{:S(2)}) collective-permute-start(f32[4,32,1024]{2,1,0:T(8,128)S(1)} %get-tuple-element.43), channel_id=1, source_target_pairs={{1,0},{2,1},{3,2},{5,4},{6,5},{7,6},{9,8},{10,9},{11,10},{13,12},{... | collective-permute-start | bytes 1572872 | tf_op jit(solution)/shard_map/ppermute | solution.py:28
  495.9 16.7 %collective-permute-start.2 = (f32[4,32,1024]{2,1,0:T(8,128)S(1)}, f32[4,32,1024]{2,1,0:T(8,128)S(1)}, u32[]{:S(2)}, u32[]{:S(2)}) collective-permute-start(f32[4,32,1024]{2,1,0:T(8,128)S(1)} %get-tuple-element.42), channel_id=1, source_target_pairs={{0,1},{1,2},{2,3},{4,5},{5,6},{6,7},{8,9},{9,10},{10,11},{12,13},{... | collective-permute-start | bytes 1572872 | tf_op jit(solution)/shard_map/ppermute | solution.py:26
  694.0 1.6 copy-start.7
  695.6 49.4 %copy-start.6 = (f32[256,1024]{0,1:T(8,128)S(1)}, f32[256,1024]{0,1:T(8,128)}, u32[]{:S(2)}) copy-start(f32[256,1024]{0,1:T(8,128)} %fusion.53) | copy-start | bytes 3145732
  746.7 1.6 copy-start.8
  748.4 48.4 %copy-start.5 = (f32[256,1024]{0,1:T(8,128)S(1)}, f32[256,1024]{0,1:T(8,128)}, u32[]{:S(2)}) copy-start(f32[256,1024]{0,1:T(8,128)} %fusion.52) | copy-start | bytes 3145732
  798.5 1.7 copy-start.9
  800.2 49.8 %copy-start.4 = (f32[256,1024]{0,1:T(8,128)S(1)}, f32[256,1024]{0,1:T(8,128)}, u32[]{:S(2)}) copy-start(f32[256,1024]{0,1:T(8,128)} %fusion.51) | copy-start | bytes 3145732
  854.4 49.5 %copy-start.1 = (f32[1,256,1024]{2,1,0:T(8,128)S(1)}, f32[1,256,1024]{2,1,0:T(8,128)}, u32[]{:S(2)}) copy-start(f32[1,256,1024]{2,1,0:T(8,128)} %copy.105) | copy-start | bytes 3145732
  854.4 49.5 %copy-start.2 = (f32[1,256,1024]{2,1,0:T(8,128)S(1)}, f32[1,256,1024]{2,1,0:T(8,128)}, u32[]{:S(2)}) copy-start(f32[1,256,1024]{2,1,0:T(8,128)} %copy.110) | copy-start | bytes 3145732
  854.4 49.5 %copy-start.3 = (f32[1,256,1024]{2,1,0:T(8,128)S(1)}, f32[1,256,1024]{2,1,0:T(8,128)}, u32[]{:S(2)}) copy-start(f32[1,256,1024]{2,1,0:T(8,128)} %copy.115) | copy-start | bytes 3145732
Sparse Core Ops, SparseCore 0:
  11.5 56.9 all-gather.1
  909.4 67.1 all-reduce.9
where the time goes:
time: 1000 us; the launch traced here: 986 us
  matrix products  731 us (73%)
  waiting for transfers between devices  120 us (12%)
  local copies, waits for them, and re-layouts  83.3 us (8%)
  other arithmetic  24.6 us (2%)
  between operations  15 us (2%)
  starting transfers between devices  12.5 us (1%)
    dot_general x8, matrix products, lateral_apply(): jnp.einsum('rnk,kc->rnc', windows, matrix, precision=lax.Precision.HIGHEST)  374 us
    unnamed x8, matrix products  356 us
    pmax x1, waiting for transfers between devices, on_device(): projection = lax.pmax(jnp.max(updated, axis=0), 'depth')  62.6 us
    all_gather x1, waiting for transfers between devices, carried_in(): gathered = lax.all_gather(part, axis)  38.1 us
    unnamed x55, local copies, waits for them, and re-layouts  36.3 us
    slice x28, local copies, waits for them, and re-layouts, band_matrix(): result = jnp.where(offsets == index, kernel[index], result)  20.4 us
  transfers between devices with their start and end apart: 6, of which 6 were waited for; matrix products, arithmetic and copies ran while one was open for 3% of the time, Pallas kernels for 0%

commit v1 on v0

v1 whole, which is shorter than its diff:
```python
import functools

import jax
import jax.numpy as jnp
from jax import lax
from jax.experimental import pallas as pl
from jax.experimental.pallas import tpu as pltpu
from jax.sharding import PartitionSpec as P

MESH = pl.DeviceIdType.MESH
BLOCK = 256
SIDE = 128


def split(value):
    high = value.astype(jnp.bfloat16)
    low = (value - high.astype(jnp.float32)).astype(jnp.bfloat16)
    return high, low


def kernel(
    dims, base_rows, base_cols, seams, meas_hbm, est_hbm, ext_hbm, upd_hbm, proj_hbm,
    meas, est, ext, local, stacked, quot, upd, vband, lhigh, llow, mhigh, mlow,
    slab, pooled, carried, sums, message, landed, above, peak, mpool, mland,
    lhalo, fhalo, qhalo,
    in_sem, out_sem, hal_send, hal_recv, q_send, q_recv, col_send, col_recv,
):
    depth_count, tile_count, planes, rows, cols, reach = dims
    half = rows // 2
    bits = depth_count.bit_length() - 1
    rest = list(range(1, bits))
    orders = [rest, rest[::-1]] if len(rest) == 2 else [rest]
    part = half // len(orders)
    steps = len(rest)
    wide = rows + 2 * reach
    chunk = 32
    d = lax.axis_index("depth")
    t = lax.axis_index("tile")
    has_up = t > 0
    has_down = t < tile_count - 1
    up = jnp.maximum(t - 1, 0)
    down = jnp.minimum(t + 1, tile_count - 1)

    def bit(b):
        return (d // (1 << b)) % 2

    def partner(b):
        return d + (1 - 2 * bit(b)) * (1 << b)

    def loads(which, src, dst):
        return pltpu.make_async_copy(src, dst, in_sem.at[which])

    get_ext = loads(0, ext_hbm, ext)
    get_est = loads(1, est_hbm, est)
    get_meas = loads(2, meas_hbm, meas)
    get_ext.start()
    get_est.start()
    get_meas.start()

    barrier = pltpu.get_barrier_semaphore()
    for b in range(bits):
        pl.semaphore_signal(barrier, inc=1, device_id={"depth": partner(b)}, device_id_type=MESH)

    @pl.when(has_up)
    def _():
        pl.semaphore_signal(barrier, inc=1, device_id={"tile": up}, device_id_type=MESH)

    @pl.when(has_down)
    def _():
        pl.semaphore_signal(barrier, inc=1, device_id={"tile": down}, device_id_type=MESH)

    def remote(src, dst, send, recv, where):
        return pltpu.make_async_remote_copy(
            src_ref=src, dst_ref=dst, send_sem=send, recv_sem=recv, device_id=where, device_id_type=MESH
        )

    def halo_pair(head, tail, to_up, to_down, send, recv):
        return (
            remote(head, to_up, send(0), recv(1), {"tile": up}),
            remote(tail, to_down, send(1), recv(0), {"tile": down}),
        )

    def halo_start(pair):
        pl.when(has_up)(lambda: pair[0].start())
        pl.when(has_down)(lambda: pair[1].start())

    def halo_recv(pair):
        pl.when(has_up)(lambda: pair[1].wait_recv())
        pl.when(has_down)(lambda: pair[0].wait_recv())

    def halo_sent(pair):
        pl.when(has_up)(lambda: pair[0].wait_send())
        pl.when(has_down)(lambda: pair[1].wait_send())

    @pl.when(t == 0)
    def _():
        lhalo[0] = jnp.zeros(lhalo.shape[1:], jnp.float32)
        fhalo[0] = jnp.zeros(fhalo.shape[1:], jnp.float32)
        qhalo[0] = jnp.zeros(qhalo.shape[1:], jnp.float32)

    @pl.when(t == tile_count - 1)
    def _():
        lhalo[1] = jnp.zeros(lhalo.shape[1:], jnp.float32)
        fhalo[1] = jnp.zeros(fhalo.shape[1:], jnp.float32)
        qhalo[1] = jnp.zeros(qhalo.shape[1:], jnp.float32)

    def over(count, body, size=chunk):
        def one(i, _):
            body(pl.ds(pl.multiple_of(i * size, size), size))
            return 0

        lax.fori_loop(0, count // size, one, 0)

    get_ext.wait()

    def slab_sum(at):
        total = ext[0, at, :]
        for p in range(1, planes):
            total = total + ext[p, at, :]
        slab[at, :] = total

    over(rows, slab_sum)
    pl.semaphore_wait(barrier, bits + has_up.astype(jnp.int32) + has_down.astype(jnp.int32))

    core = bit(0)
    own = pl.multiple_of(core * half, half)
    other = pl.multiple_of((1 - core) * half, half)

    rs = remote(slab.at[pl.ds(other, half)], pooled, col_send.at[0], col_recv.at[0], {"depth": partner(0)})
    rs.start()
    get_est.wait()

    def local_weights(at):
        run = jnp.zeros((chunk, cols), jnp.float32)
        for p in range(planes):
            local[p, at, :] = jnp.exp(-run) * est[p, at, :]
            if p < planes - 1:
                run = run + ext[p, at, :]

    over(rows, local_weights)
    lpair = halo_pair(
        local.at[:, pl.ds(0, reach)], local.at[:, pl.ds(rows - reach, reach)], lhalo.at[1], lhalo.at[0],
        lambda i: hal_send.at[i], lambda i: hal_recv.at[i],
    )
    halo_start(lpair)
    rs.wait_recv()

    def pool(at):
        sums[at, :] = slab[pl.ds(own + at.start, chunk), :] + pooled[at, :]

    over(half, pool)

    hops = []
    for s in range(steps):
        row = []
        for g, order in enumerate(orders):
            where = pl.ds(g * part, part)
            at = 2 + s * len(orders) + g
            row.append(remote(
                message.at[s - 1, where] if s else sums.at[where], landed.at[s, where],
                col_send.at[at], col_recv.at[at], {"depth": partner(order[s])},
            ))
        hops.append(row)
    for hop in hops[0]:
        hop.start()

    up_flag = jnp.where(has_up, seams[up], 0).astype(jnp.float32)
    down_flag = jnp.where(has_down, seams[jnp.minimum(t, tile_count - 2)], 0).astype(jnp.float32)
    lane = lax.broadcasted_iota(jnp.int32, (rows, 4 * BLOCK), 1)
    third = jnp.where(lane < wide, lane, jnp.where(lane < 2 * wide, lane - wide, lane - 2 * wide))
    scale = jnp.where(third < reach, up_flag, jnp.where(third >= wide - reach, down_flag, 1.0))

    def bands(i, _):
        tall = jnp.broadcast_to(base_rows[i], (rows, 4 * BLOCK))
        tall = pltpu.roll(tall, 0, 1, stride=1, stride_axis=0) * scale
        high, low = split(tall)
        vband[i] = jnp.where(lane < 2 * wide, high.astype(jnp.float32), low.astype(jnp.float32)).astype(jnp.bfloat16)
        square = jnp.broadcast_to(base_cols[i], (2 * BLOCK, 2 * BLOCK))
        square = pltpu.roll(square, 0, 1, stride=1, stride_axis=0)[:, :BLOCK]
        high, low = split(square)
        lhigh[i] = high
        llow[i] = low
        return 0

    lax.fori_loop(0, 2 * planes, bands, 0)
    for m in (mhigh, mlow):
        m[:, :SIDE] = jnp.zeros((rows, SIDE), jnp.bfloat16)
        m[:, SIDE + cols:] = jnp.zeros((rows, SIDE), jnp.bfloat16)

    for s in range(steps):
        for g, order in enumerate(orders):
            hops[s][g].wait_recv()
            upper = bit(order[s]).astype(jnp.float32)
            ascending = s == 0 or order[s] > order[s - 1]

            def absorb(at, s=s, g=g, order=order, upper=upper, ascending=ascending):
                at = pl.ds(g * part + at.start, chunk)
                got = landed[s, at, :]
                if s == 0:
                    before = upper * got
                elif ascending:
                    before = carried[at, :] + upper * got
                else:
                    before = carried[at, :] + got
                carried[at, :] = before
                if s + 1 < steps:
                    if order[s + 1] > order[s]:
                        total = (sums[at, :] if s == 0 else message[s - 1, at, :]) + got
                        message[s, at, :] = total
                    else:
                        lower = 1.0 - bit(order[s + 1]).astype(jnp.float32)
                        message[s, at, :] = before + lower * sums[at, :]

            over(part, absorb)
            if s + 1 < steps:
                hops[s + 1][g].start()

    ag = remote(slab.at[pl.ds(own, half)], above.at[pl.ds(own, half)], col_send.at[1], col_recv.at[1], {"depth": partner(0)})
    first = core.astype(jnp.float32)

    def give(at):
        rest_at = pl.ds(own + at.start, chunk)
        before = carried[at, :]
        above[rest_at, :] = before + first * pooled[at, :]
        slab[rest_at, :] = before + (1.0 - first) * slab[rest_at, :]

    over(half, give)
    ag.start()
    ag.wait_recv()

    def fade(at):
        above[at, :] = jnp.exp(-above[at, :])

    over(rows, fade)
    fpair = halo_pair(
        above.at[pl.ds(0, reach)], above.at[pl.ds(rows - reach, reach)], fhalo.at[1], fhalo.at[0],
        lambda i: hal_send.at[2 + i], lambda i: hal_recv.at[2 + i],
    )
    halo_start(fpair)
    get_meas.wait()
    halo_recv(lpair)
    halo_recv(fpair)

    def put(value, start, size):
        high, low = split(value)
        stacked[pl.ds(start, size), :] = high
        stacked[pl.ds(wide + start, size), :] = low
        stacked[pl.ds(2 * wide + start, size), :] = high

    def blur(i, use):
        for n in range(cols // BLOCK):
            mixed = jnp.dot(
                vband[i, :, : 3 * wide], stacked[:, n * BLOCK : (n + 1) * BLOCK], preferred_element_type=jnp.float32
            )
            high, low = split(mixed)
            mhigh[:, SIDE + n * BLOCK : SIDE + (n + 1) * BLOCK] = high
            mlow[:, SIDE + n * BLOCK : SIDE + (n + 1) * BLOCK] = low
        for n in range(cols // BLOCK):
            def window(m):
                start = n * BLOCK
                return jnp.concatenate(
                    [m[:, start + SIDE : start + SIDE + BLOCK + SIDE], m[:, start : start + SIDE]], axis=1
                )

            high, low = window(mhigh), window(mlow)
            use(
                slice(n * BLOCK, (n + 1) * BLOCK),
                jnp.dot(high, lhigh[i], preferred_element_type=jnp.float32)
                + jnp.dot(low, lhigh[i], preferred_element_type=jnp.float32)
                + jnp.dot(high, llow[i], preferred_element_type=jnp.float32),
            )

    def qpair_of(p):
        return halo_pair(
            quot.at[p, pl.ds(0, reach)], quot.at[p, pl.ds(rows - reach, reach)], qhalo.at[1, p], qhalo.at[0, p],
            lambda i: q_send.at[i, p], lambda i: q_recv.at[i, p],
        )

    def forward(p, _):
        put(fhalo[0] * lhalo[0, p], 0, reach)
        put(fhalo[1] * lhalo[1, p], rows + reach, reach)

        def inner(at):
            put(above[at, :] * local[p, at, :], pl.multiple_of(at.start + reach, chunk), chunk)

        over(rows, inner)

        def use(at, blurred):
            quot[p, :, at] = meas[p, :, at] / blurred

        blur(p, use)
        halo_start(qpair_of(p))
        return 0

    lax.fori_loop(0, planes, forward, 0)

    def backward(p, _):
        halo_recv(qpair_of(p))
        put(qhalo[0, p], 0, reach)
        put(qhalo[1, p], rows + reach, reach)

        def inner(at):
            put(quot[p, at, :], pl.multiple_of(at.start + reach, chunk), chunk)

        over(rows, inner)

        def use(at, spread):
            upd[p, :, at] = est[p, :, at] * spread

        blur(planes + p, use)
        pltpu.make_async_copy(upd.at[p], upd_hbm.at[p], out_sem.at[p]).start()
        return 0

    lax.fori_loop(0, planes, backward, 0)

    def top(at):
        best = upd[0, at, :]
        for p in range(1, planes):
            best = jnp.maximum(best, upd[p, at, :])
        peak[at, :] = best

    over(rows, top)
    base = 2 + steps * len(orders)
    rs2 = remote(peak.at[pl.ds(other, half)], mpool.at[0], col_send.at[base], col_recv.at[base], {"depth": partner(0)})
    rs2.start()
    rs2.wait_recv()

    def merge(at):
        mpool[1, at, :] = jnp.maximum(mpool[0, at, :], peak[pl.ds(own + at.start, chunk), :])

    over(half, merge)
    hops2 = []
    for s in range(steps):
        row = []
        for g, order in enumerate(orders):
            where = pl.ds(g * part, part)
            at = base + 2 + s * len(orders) + g
            row.append(remote(
                mpool.at[1 + s, where], mland.at[s, where], col_send.at[at], col_recv.at[at],
                {"depth": partner(order[s])},
            ))
        hops2.append(row)
    for hop in hops2[0]:
        hop.start()
    for s in range(steps):
        for g in range(len(orders)):
            hops2[s][g].wait_recv()

            def keep(at, s=s, g=g):
                at = pl.ds(g * part + at.start, chunk)
                mpool[2 + s, at, :] = jnp.maximum(mpool[1 + s, at, :], mland[s, at, :])

            over(part, keep)
            if s + 1 < steps:
                hops2[s + 1][g].start()
    ag2 = remote(mpool.at[1 + steps], mland.at[steps], col_send.at[base + 1], col_recv.at[base + 1], {"depth": partner(0)})
    ag2.start()
    put_own = pltpu.make_async_copy(mpool.at[1 + steps], proj_hbm.at[pl.ds(own, half)], out_sem.at[planes])
    put_own.start()
    ag2.wait_recv()
    put_other = pltpu.make_async_copy(mland.at[steps], proj_hbm.at[pl.ds(other, half)], out_sem.at[planes + 1])
    put_other.start()

    rs.wait_send()
    ag.wait_send()
    rs2.wait_send()
    ag2.wait_send()
    for row in hops + hops2:
        for hop in row:
            hop.wait_send()
    halo_sent(lpair)
    halo_sent(fpair)
    for p in range(planes):
        halo_sent(qpair_of(p))
        pltpu.make_async_copy(upd.at[p], upd_hbm.at[p], out_sem.at[p]).wait()
    put_own.wait()
    put_other.wait()


def on_device(dims, measured, estimate, extinction, psf_rows, psf_cols, stratum, seam_flags):
    depth_count, tile_count, planes, rows, cols, reach = dims
    strata, length = psf_rows.shape
    wide = rows + 2 * reach
    picker = (stratum[:, None] == jnp.arange(strata, dtype=jnp.int32)[None, :])[:, :, None]

    def choose(psf):
        taps = psf / jnp.sum(psf, axis=1, keepdims=True)
        return jnp.sum(jnp.where(picker, taps[None], 0.0), axis=1)

    vertical, lateral = choose(psf_rows), choose(psf_cols)
    vertical = jnp.concatenate([vertical, vertical[:, ::-1]], axis=0)
    lateral = jnp.concatenate([lateral[:, ::-1], lateral], axis=0)
    third = jnp.pad(vertical, ((0, 0), (0, wide - length)))
    base_rows = jnp.pad(jnp.concatenate([third] * 3, axis=1), ((0, 0), (0, 4 * BLOCK - 3 * wide)))[:, None, :]
    gap = jnp.zeros((2 * planes, 2 * BLOCK - length), jnp.float32)
    base_cols = jnp.concatenate([lateral[:, reach:], gap, lateral[:, :reach]], axis=1)[:, None, :]

    half = rows // 2
    bits = depth_count.bit_length() - 1
    steps = bits - 1
    groups = 2 if steps == 2 else 1
    collectives = 2 * (2 + steps * groups)
    f32, bf16 = jnp.float32, jnp.bfloat16
    whole = (planes, rows, cols)
    return pl.pallas_call(
        functools.partial(kernel, dims),
        out_shape=(jax.ShapeDtypeStruct(whole, f32), jax.ShapeDtypeStruct((rows, cols), f32)),
        in_specs=[
            pl.BlockSpec(memory_space=pltpu.VMEM),
            pl.BlockSpec(memory_space=pltpu.VMEM),
            pl.BlockSpec(memory_space=pltpu.SMEM),
            pl.BlockSpec(memory_space=pl.ANY),
            pl.BlockSpec(memory_space=pl.ANY),
            pl.BlockSpec(memory_space=pl.ANY),
        ],
        out_specs=(pl.BlockSpec(memory_space=pl.ANY), pl.BlockSpec(memory_space=pl.ANY)),
        scratch_shapes=[
            pltpu.VMEM(whole, f32),
            pltpu.VMEM(whole, f32),
            pltpu.VMEM(whole, f32),
            pltpu.VMEM(whole, f32),
            pltpu.VMEM((3 * wide, cols), bf16),
            pltpu.VMEM(whole, f32),
            pltpu.VMEM(whole, f32),
            pltpu.VMEM((2 * planes, rows, 4 * BLOCK), bf16),
            pltpu.VMEM((2 * planes, 2 * BLOCK, BLOCK), bf16),
            pltpu.VMEM((2 * planes, 2 * BLOCK, BLOCK), bf16),
            pltpu.VMEM((rows, cols + 2 * SIDE), bf16),
            pltpu.VMEM((rows, cols + 2 * SIDE), bf16),
            pltpu.VMEM((rows, cols), f32),
            pltpu.VMEM((half, cols), f32),
            pltpu.VMEM((half, cols), f32),
            pltpu.VMEM((half, cols), f32),
            pltpu.VMEM((max(steps - 1, 1), half, cols), f32),
            pltpu.VMEM((steps, half, cols), f32),
            pltpu.VMEM((rows, cols), f32),
            pltpu.VMEM((rows, cols), f32),
            pltpu.VMEM((2 + steps, half, cols), f32),
            pltpu.VMEM((1 + steps, half, cols), f32),
            pltpu.VMEM((2, planes, reach, cols), f32),
            pltpu.VMEM((2, reach, cols), f32),
            pltpu.VMEM((2, planes, reach, cols), f32),
            pltpu.SemaphoreType.DMA((3,)),
            pltpu.SemaphoreType.DMA((planes + 2,)),
            pltpu.SemaphoreType.DMA((4,)),
            pltpu.SemaphoreType.DMA((4,)),
            pltpu.SemaphoreType.DMA((2, planes)),
            pltpu.SemaphoreType.DMA((2, planes)),
            pltpu.SemaphoreType.DMA((collectives,)),
            pltpu.SemaphoreType.DMA((collectives,)),
        ],
        compiler_params=pltpu.CompilerParams(
            collective_id=0, has_side_effects=True, vmem_limit_bytes=62 * 1024 * 1024
        ),
    )(base_rows, base_cols, seam_flags, measured, estimate, extinction)


def solution(mesh):
    def body(measured, estimate, extinction, psf_rows, psf_cols, stratum, seam_flags):
        planes, rows, cols = measured.shape
        dims = (mesh.shape["depth"], mesh.shape["tile"], planes, rows, cols, (psf_rows.shape[1] - 1) // 2)
        return on_device(dims, measured, estimate, extinction, psf_rows, psf_cols, stratum, seam_flags)

    return jax.shard_map(
        body,
        mesh=mesh,
        in_specs=(
            P("depth", "tile", None),
            P("depth", "tile", None),
            P("depth", "tile", None),
            P(),
            P(),
            P("depth"),
            P(),
        ),
        out_specs=(P("depth", "tile", None), P("tile", None)),
        check_vma=False,
    )
```

time: 1000 us -> 78 us (0.08); the launches traced: 986 us -> 77 us
  matrix products: 731 us -> 0 us
  waiting for transfers between devices: 120 us -> 0 us
  local copies, waits for them, and re-layouts: 83.3 us -> 7.45 us
  Pallas kernels: 0 us -> 65.4 us
  other arithmetic: 24.6 us -> 3.41 us
  between operations: 15 us -> 0.66 us
  starting transfers between devices: 12.5 us -> 0 us
    dot_general x10 -> x0, matrix products: 375 us -> none  [the longest x8 374 us: lateral_apply(): jnp.einsum('rnk,kc->rnc', windows, matrix, precision=lax.Precision.HIGHEST)]
    unnamed x8 -> x0, matrix products: 356 us -> none
    pallas_call x0 -> x1, Pallas kernels: none -> 65.4 us  [on_device(): pl.pallas_call(functools.partial(kernel, dims), out_shape=(jax.ShapeDtype...]
    pmax x1 -> x0, waiting for transfers between devices: 62.6 us -> none  [on_device(): projection = lax.pmax(jnp.max(updated, axis=0), 'depth')]
    all_gather x1 -> x0, waiting for transfers between devices: 38.1 us -> none  [carried_in(): gathered = lax.all_gather(part, axis)]
    unnamed x55 -> x4, local copies, waits for them, and re-layouts: 36.3 us -> 5.85 us
    slice x38 -> x1, local copies, waits for them, and re-layouts: 27.6 us -> 0.07 us  [on_device(): lateral[:, reach:]]
    ppermute x4 -> x0, waiting for transfers between devices: 18.9 us -> none  [the longest x2 16 us: with_halo(): lax.ppermute(head, axis, [((i + 1) % count, i) for i in range(ends)])]
  transfers between devices with their start and end apart: 6 -> 0, of which waited for: 6 -> 0; matrix products, arithmetic and copies ran while one was open for 3% -> 0% of each run, Pallas kernels for 0% -> 0%
where the time goes in v1:
time: 78 us; the launch traced here: 77 us
  Pallas kernels  65.4 us (84%)
  local copies, waits for them, and re-layouts  7.45 us (10%)
  other arithmetic  3.41 us (4%)
    pallas_call x1, Pallas kernels, on_device(): pl.pallas_call(functools.partial(kernel, dims), out_shape=(jax.ShapeDtype...  65.4 us
    unnamed x4, local copies, waits for them, and re-layouts  5.85 us
    reduce_sum x2, other arithmetic, choose(): taps = psf / jnp.sum(psf, axis=1, keepdims=True)  1.63 us

profile of v1, /device:TPU:0, one launch (start us, length us, event | category | flops | bytes accessed | tf_op | source)
XLA Modules:
  0.0 77.0 jit_solution(16845598361990441121)
XLA Ops:
  0.6 0.7 iota_compare_fusion.2
  1.4 0.8 %reduce_sum.36 = f32[16]{0:T(128)S(1)} reduce(f32[16,65]{1,0:T(8,128)} %param.10, f32[]{:T(128)} %constant.1.clone.1), dimensions={1}, to_apply=%region_0.0 | reduce | flops 1024 | bytes 4228 | tf_op jit(solution)/shard_map/reduce_sum | solution.py:387
  2.2 0.8 %reduce_sum.38 = f32[16]{0:T(128)S(1)} reduce(f32[16,65]{1,0:T(8,128)} %param.11, f32[]{:T(128)} %constant.1.clone.1), dimensions={1}, to_apply=%region_2.3 | reduce | flops 1024 | bytes 4228 | tf_op jit(solution)/shard_map/reduce_sum | solution.py:387
  3.0 0.1 pad.11.clone
  3.1 0.8 %broadcast_divide_fusion = (f32[16,65]{1,0:T(8,128)S(1)}, f32[16,65]{1,0:T(8,128)S(1)}) fusion(f32[16,65]{1,0:T(8,128)} %param.11, f32[16]{0:T(128)S(1)} %reduce_sum.38, f32[16,65]{1,0:T(8,128)} %param.10, f32[16]{0:T(128)S(1)} %reduce_sum.36), kind=kLoop, calls=%fused_computation.9 | loop fusion | flops 2080 | bytes 16768 | tf_op jit(solution)/shard_map/div | solution.py:387
  3.9 0.1 select_reduce_fusion
  4.0 0.1 rev.7
  4.1 0.1 rev.6
  4.2 0.1 slice.6
  4.2 0.1 pad_maximum_fusion
  4.3 0.6 broadcast_in_dim.51.base_cols
  4.9 0.1 select_maximum_fusion
  5.0 0.6 broadcast_in_dim.48.base_rows
  5.7 65.4 %shard_map.86 = (f32[4,256,1024]{2,1,0:T(8,128)}, f32[256,1024]{1,0:T(8,128)}) custom-call(f32[8,1,1024]{2,1,0:T(1,128)} %broadcast_in_dim.48.base_rows, f32[8,1,512]{2,1,0:T(1,128)} %broadcast_in_dim.51.base_cols, s32[3]{0:T(128)} %seams.1, f32[4,256,1024]{2,1,0:T(8,128)} %meas_hbm.1, f32[4,256,1024]{2,1,0:T(8,128)} %est_hbm.1, f32[4,256,1024]{2,1,0:T(8,128)} %ext_hbm.1), custom_call_target="tpu_custom_call" | custom-call | tf_op jit(solution)/shard_map/pallas_call | solution.py:405
  71.1 0.0 copy-start
  71.1 4.9 %copy.11 = f32[4,256,1024]{2,1,0:T(8,128)} copy(f32[4,256,1024]{2,1,0:T(8,128)} %get-tuple-element.8) | data formatting | bytes 8388608
  76.0 0.0 copy-done
  76.0 1.0 %copy.12 = f32[256,1024]{1,0:T(8,128)} copy(f32[256,1024]{1,0:T(8,128)S(1)} %copy-done) | data formatting | bytes 2097152
  (3 shorter events, 0.0 us)
Async XLA Ops:
  71.1 4.9 %copy-start = (f32[256,1024]{1,0:T(8,128)S(1)}, f32[256,1024]{1,0:T(8,128)}, u32[]{:S(2)}) copy-start(f32[256,1024]{1,0:T(8,128)} %get-tuple-element.9) | copy-start | bytes 3145732

commit v2 on v1

v2 whole, which is shorter than its diff:
```python
import functools

import jax
import jax.numpy as jnp
from jax import lax
from jax.experimental import pallas as pl
from jax.experimental.pallas import tpu as pltpu
from jax.sharding import PartitionSpec as P

MESH = pl.DeviceIdType.MESH
BLOCK = 256
SIDE = 128


def split(value):
    high = value.astype(jnp.bfloat16)
    low = (value - high.astype(jnp.float32)).astype(jnp.bfloat16)
    return high, low


def kernel(
    dims, psf_rows, psf_cols, stratum, seams, meas_hbm, est_hbm, ext_hbm, upd, proj,
    meas, est, ext, local, stacked, tall_table, flat_table, vband, lhigh, llow, mhigh, mlow,
    slab, pooled, carried, sums, message, landed, above, peak, mpool, mland,
    lhalo, fhalo, qhalo,
    in_sem, hal_send, hal_recv, q_send, q_recv, col_send, col_recv,
):
    depth_count, tile_count, planes, rows, cols, reach = dims
    half = rows // 2
    bits = depth_count.bit_length() - 1
    rest = list(range(1, bits))
    orders = [rest, rest[::-1]] if len(rest) == 2 else [rest]
    part = half // len(orders)
    steps = len(rest)
    wide = rows + 2 * reach
    chunk = 64
    blocks = cols // BLOCK
    groups = len(orders)
    d = lax.axis_index("depth")
    t = lax.axis_index("tile")
    has_up = t > 0
    has_down = t < tile_count - 1
    up = jnp.maximum(t - 1, 0)
    down = jnp.minimum(t + 1, tile_count - 1)

    def bit(b):
        return (d // (1 << b)) % 2

    def partner(b):
        return d + (1 - 2 * bit(b)) * (1 << b)

    def loads(which, src, dst):
        return pltpu.make_async_copy(src, dst, in_sem.at[which])

    def span(n):
        return pl.ds(n * BLOCK, BLOCK)

    get_ext = [loads(2 + n, ext_hbm.at[:, :, span(n)], ext.at[:, :, span(n)]) for n in range(blocks)]
    get_est = loads(0, est_hbm, est)
    get_meas = loads(1, meas_hbm, meas)
    for n in range(blocks):
        get_ext[n].start()
    get_est.start()
    get_meas.start()

    barrier = pltpu.get_barrier_semaphore()
    for b in range(bits):
        pl.semaphore_signal(barrier, inc=1, device_id={"depth": partner(b)}, device_id_type=MESH)

    @pl.when(has_up)
    def _():
        pl.semaphore_signal(barrier, inc=1, device_id={"tile": up}, device_id_type=MESH)

    @pl.when(has_down)
    def _():
        pl.semaphore_signal(barrier, inc=1, device_id={"tile": down}, device_id_type=MESH)

    def remote(src, dst, send, recv, where):
        return pltpu.make_async_remote_copy(
            src_ref=src, dst_ref=dst, send_sem=send, recv_sem=recv, device_id=where, device_id_type=MESH
        )

    def halo_pair(head, tail, to_up, to_down, send, recv):
        return (
            remote(head, to_up, send(0), recv(1), {"tile": up}),
            remote(tail, to_down, send(1), recv(0), {"tile": down}),
        )

    def halo_start(pair):
        pl.when(has_up)(lambda: pair[0].start())
        pl.when(has_down)(lambda: pair[1].start())

    def halo_recv(pair):
        pl.when(has_up)(lambda: pair[1].wait_recv())
        pl.when(has_down)(lambda: pair[0].wait_recv())

    def halo_sent(pair):
        pl.when(has_up)(lambda: pair[0].wait_send())
        pl.when(has_down)(lambda: pair[1].wait_send())

    @pl.when(t == 0)
    def _():
        lhalo[0] = jnp.zeros(lhalo.shape[1:], jnp.float32)
        fhalo[0] = jnp.zeros(fhalo.shape[1:], jnp.float32)
        qhalo[0] = jnp.zeros(qhalo.shape[1:], jnp.float32)

    @pl.when(t == tile_count - 1)
    def _():
        lhalo[1] = jnp.zeros(lhalo.shape[1:], jnp.float32)
        fhalo[1] = jnp.zeros(fhalo.shape[1:], jnp.float32)
        qhalo[1] = jnp.zeros(qhalo.shape[1:], jnp.float32)

    def over(count, body, size=chunk):
        def one(i, _):
            body(pl.ds(pl.multiple_of(i * size, size), size))
            return 0

        lax.fori_loop(0, count // size, one, 0)

    core = bit(0)
    own = pl.multiple_of(core * half, half)
    other = pl.multiple_of((1 - core) * half, half)
    first = core.astype(jnp.float32)

    class Exchange:
        def __init__(self, base, source, mine, pooled, lead, relay, landed, finish, target):
            self.base = base
            self.rs = [self.copy(0, n, source.at[pl.ds(other, half), span(n)], pooled.at[:, span(n)], 0) for n in range(blocks)]
            self.hops = []
            for s in range(steps):
                level = []
                for n in range(blocks):
                    row = []
                    for g, order in enumerate(orders):
                        where = pl.ds(g * part, part)
                        src = relay.at[s - 1, where, span(n)] if s else lead.at[where, span(n)]
                        row.append(self.copy(2 + s * groups + g, n, src, landed.at[s, where, span(n)], order[s]))
                    level.append(row)
                self.hops.append(level)
            self.ag = [self.copy(1, n, finish(n), target.at[pl.ds(own, half), span(n)], 0) for n in range(blocks)]

        def copy(self, slot, n, src, dst, b):
            at = self.base + slot
            return remote(src, dst, col_send.at[at, n], col_recv.at[at, n], {"depth": partner(b)})

        def sent(self):
            for n in range(blocks):
                self.rs[n].wait_send()
                self.ag[n].wait_send()
                for level in self.hops:
                    for hop in level[n]:
                        hop.wait_send()

    prefix = Exchange(0, slab, own, pooled, sums, message, landed, lambda n: slab.at[pl.ds(own, half), span(n)], above)
    maxima = Exchange(
        2 + steps * groups, peak, own, mpool.at[0], mpool.at[1], mpool.at[pl.ds(2, steps)], mland,
        lambda n: mpool.at[1 + steps, :, span(n)], proj,
    )

    for n in range(blocks):
        get_ext[n].wait()

        def slab_sum(at, n=n):
            total = ext[0, at, span(n)]
            for p in range(1, planes):
                total = total + ext[p, at, span(n)]
            slab[at, span(n)] = total

        over(rows, slab_sum)
        if n == 0:
            pl.semaphore_wait(barrier, bits + has_up.astype(jnp.int32) + has_down.astype(jnp.int32))
        prefix.rs[n].start()

    for n in range(blocks):
        prefix.rs[n].wait_recv()

        def pool(at, n=n):
            sums[at, span(n)] = slab[pl.ds(own + at.start, chunk), span(n)] + pooled[at, span(n)]

        over(half, pool)
        for hop in prefix.hops[0][n]:
            hop.start()

    get_est.wait()

    def local_weights(at):
        run = ext[0, at, :]
        local[0, at, :] = est[0, at, :]
        for p in range(1, planes):
            local[p, at, :] = jnp.exp(-run) * est[p, at, :]
            if p < planes - 1:
                run = run + ext[p, at, :]

    over(rows, local_weights, 32)
    lpair = halo_pair(
        local.at[:, pl.ds(0, reach)], local.at[:, pl.ds(rows - reach, reach)], lhalo.at[1], lhalo.at[0],
        lambda i: hal_send.at[i], lambda i: hal_recv.at[i],
    )
    halo_start(lpair)

    strata, length = psf_rows.shape
    highest = lax.Precision.HIGHEST

    def spread_taps(psf, width, place):
        taps = psf[...] / jnp.sum(psf[...], axis=1, keepdims=True)
        tap = lax.broadcasted_iota(jnp.int32, (length, width), 0)
        lane = lax.broadcasted_iota(jnp.int32, (length, width), 1)
        pick = place(tap, lane).astype(jnp.float32)
        return jnp.dot(taps, pick, preferred_element_type=jnp.float32, precision=highest)

    def thirds(tap, lane):
        return (lane == tap) | (lane == tap + wide) | (lane == tap + 2 * wide)

    tall_table[0] = spread_taps(psf_rows, 4 * BLOCK, thirds)
    tall_table[1] = spread_taps(psf_rows, 4 * BLOCK, lambda tap, lane: thirds(length - 1 - tap, lane))

    def around(tap, lane):
        return lane == jnp.where(tap >= reach, tap - reach, tap - reach + 2 * BLOCK)

    flat_table[0] = spread_taps(psf_cols, 2 * BLOCK, lambda tap, lane: around(length - 1 - tap, lane))
    flat_table[1] = spread_taps(psf_cols, 2 * BLOCK, around)

    up_flag = jnp.where(has_up, seams[up], 0).astype(jnp.float32)
    down_flag = jnp.where(has_down, seams[jnp.minimum(t, tile_count - 2)], 0).astype(jnp.float32)
    lane = lax.broadcasted_iota(jnp.int32, (1, 4 * BLOCK), 1)
    third = jnp.where(lane < wide, lane, jnp.where(lane < 2 * wide, lane - wide, lane - 2 * wide))
    scale = jnp.where(third < reach, up_flag, jnp.where(third >= wide - reach, down_flag, 1.0))

    def bands(which):
        def one(p, _):
            i = which * planes + p
            row = stratum[p]
            tall = jnp.broadcast_to(tall_table[which, pl.ds(row, 1), :], (rows, 4 * BLOCK))
            tall = pltpu.roll(tall, 0, 1, stride=1, stride_axis=0) * scale
            high, low = split(tall)
            vband[i] = jnp.where(lane < 2 * wide, high.astype(jnp.float32), low.astype(jnp.float32)).astype(jnp.bfloat16)
            square = jnp.broadcast_to(flat_table[which, pl.ds(row, 1), :], (2 * BLOCK, 2 * BLOCK))
            square = pltpu.roll(square, 0, 1, stride=1, stride_axis=0)[:, :BLOCK]
            high, low = split(square)
            lhigh[i] = high
            llow[i] = low
            return 0

        lax.fori_loop(0, planes, one, 0)

    def absorb_all(s, n):
        for g, order in enumerate(orders):
            prefix.hops[s][n][g].wait_recv()
            upper = bit(order[s]).astype(jnp.float32)
            ascending = s == 0 or order[s] > order[s - 1]

            def absorb(at, g=g, order=order, upper=upper, ascending=ascending):
                at = pl.ds(g * part + at.start, chunk)
                got = landed[s, at, span(n)]
                if s == 0:
                    before = upper * got
                elif ascending:
                    before = carried[at, span(n)] + upper * got
                else:
                    before = carried[at, span(n)] + got
                carried[at, span(n)] = before
                if s + 1 < steps:
                    if order[s + 1] > order[s]:
                        total = (sums[at, span(n)] if s == 0 else message[s - 1, at, span(n)]) + got
                        message[s, at, span(n)] = total
                    else:
                        lower = 1.0 - bit(order[s + 1]).astype(jnp.float32)
                        message[s, at, span(n)] = before + lower * sums[at, span(n)]

            over(part, absorb)
            if s + 1 < steps:
                prefix.hops[s + 1][n][g].start()

    bands(0)
    for m in (mhigh, mlow):
        m[:, :, :SIDE] = jnp.zeros((planes, rows, SIDE), jnp.bfloat16)
        m[:, :, SIDE + cols:] = jnp.zeros((planes, rows, SIDE), jnp.bfloat16)
    for s in range(steps - 1):
        for n in range(blocks):
            absorb_all(s, n)
    bands(1)

    fpairs = [
        halo_pair(
            above.at[pl.ds(0, reach), span(n)], above.at[pl.ds(rows - reach, reach), span(n)],
            fhalo.at[1, :, span(n)], fhalo.at[0, :, span(n)],
            lambda i, n=n: hal_send.at[2 + 2 * n + i], lambda i, n=n: hal_recv.at[2 + 2 * n + i],
        )
        for n in range(blocks)
    ]

    def share(n):
        absorb_all(steps - 1, n)

        def give(at):
            mine = pl.ds(own + at.start, chunk)
            before = carried[at, span(n)]
            above[mine, span(n)] = before + first * pooled[at, span(n)]
            slab[mine, span(n)] = before + (1.0 - first) * slab[mine, span(n)]

        over(half, give)
        prefix.ag[n].start()

    def fade(n):
        prefix.ag[n].wait_recv()

        def one(at):
            above[at, span(n)] = jnp.exp(-above[at, span(n)])

        over(rows, one)
        halo_start(fpairs[n])

    def put(value, start, size):
        high, low = split(value)
        stacked[pl.ds(start, size), :] = high
        stacked[pl.ds(wide + start, size), :] = low
        stacked[pl.ds(2 * wide + start, size), :] = high

    def mix(n, which, edge, inner):
        def one(p, _):
            put(edge(0, p), 0, reach)
            put(edge(1, p), rows + reach, reach)
            over(rows, lambda at: put(inner(p, at), pl.multiple_of(at.start + reach, 32), chunk))
            mixed = jnp.dot(vband[which * planes + p, :, : 3 * wide], stacked[...], preferred_element_type=jnp.float32)
            high, low = split(mixed)
            mhigh[p, :, SIDE + n * BLOCK : SIDE + (n + 1) * BLOCK] = high
            mlow[p, :, SIDE + n * BLOCK : SIDE + (n + 1) * BLOCK] = low
            return 0

        lax.fori_loop(0, planes, one, 0)

    def blurred(n, i, p):
        def window(m):
            start = n * BLOCK
            return jnp.concatenate(
                [m[p, :, start + SIDE : start + SIDE + BLOCK + SIDE], m[p, :, start : start + SIDE]], axis=1
            )

        high, low = window(mhigh), window(mlow)
        return (
            jnp.dot(high, lhigh[i], preferred_element_type=jnp.float32)
            + jnp.dot(low, lhigh[i], preferred_element_type=jnp.float32)
            + jnp.dot(high, llow[i], preferred_element_type=jnp.float32)
        )

    quot = ext

    qpairs = [
        halo_pair(
            quot.at[:, pl.ds(0, reach), span(n)], quot.at[:, pl.ds(rows - reach, reach), span(n)],
            qhalo.at[1, :, :, span(n)], qhalo.at[0, :, :, span(n)],
            lambda i, n=n: q_send.at[i, n], lambda i, n=n: q_recv.at[i, n],
        )
        for n in range(blocks)
    ]

    def forward_mix(n):
        halo_recv(fpairs[n])
        mix(
            n, 0, lambda side, p: fhalo[side, :, span(n)] * lhalo[side, p, :, span(n)],
            lambda p, at: above[at, span(n)] * local[p, at, span(n)],
        )

    def forward_end(n):
        def one(p, _):
            quot[p, :, span(n)] = meas[p, :, span(n)] / blurred(n, p, p)
            return 0

        lax.fori_loop(0, planes, one, 0)
        halo_start(qpairs[n])

    def backward_mix(n):
        halo_recv(qpairs[n])
        mix(n, 1, lambda side, p: qhalo[side, p, :, span(n)], lambda p, at: quot[p, at, span(n)])

    def backward_end(n):
        def one(p, _):
            upd[p, :, span(n)] = est[p, :, span(n)] * blurred(n, planes + p, p)
            return 0

        lax.fori_loop(0, planes, one, 0)

        def top(at):
            best = upd[0, at, span(n)]
            for p in range(1, planes):
                best = jnp.maximum(best, upd[p, at, span(n)])
            peak[at, span(n)] = best

        over(rows, top)
        maxima.rs[n].start()

    share(0)
    for n in range(1, blocks):
        share(n)
        fade(n - 1)
    fade(blocks - 1)
    get_meas.wait()
    halo_recv(lpair)
    forward_mix(0)
    for n in range(1, blocks):
        forward_mix(n)
        forward_end(n - 1)
    forward_end(blocks - 1)

    def raise_up(k, n):
        if k == 0:
            maxima.rs[n].wait_recv()

            def merge(at):
                mpool[1, at, span(n)] = jnp.maximum(mpool[0, at, span(n)], peak[pl.ds(own + at.start, chunk), span(n)])

            over(half, merge)
            for hop in maxima.hops[0][n]:
                hop.start()
            return
        s = k - 1
        for g in range(groups):
            maxima.hops[s][n][g].wait_recv()

            def keep(at, g=g):
                at = pl.ds(g * part + at.start, chunk)
                best = jnp.maximum(mpool[1 + s, at, span(n)], mland[s, at, span(n)])
                if s + 1 < steps:
                    mpool[2 + s, at, span(n)] = best
                else:
                    mpool[1 + steps, at, span(n)] = best
                    proj[pl.ds(own + at.start, chunk), span(n)] = best

            over(part, keep)
            if s + 1 < steps:
                maxima.hops[s + 1][n][g].start()
        if s + 1 == steps:
            maxima.ag[n].start()

    backward_mix(0)
    for n in range(1, blocks + steps + 1):
        if n < blocks:
            backward_mix(n)
        for k in range(steps, -1, -1):
            if 0 <= n - 2 - k < blocks:
                raise_up(k, n - 2 - k)
        if n <= blocks:
            backward_end(n - 1)
    for k in range(steps, -1, -1):
        n = blocks + steps - 1 - k
        if n < blocks:
            raise_up(k, n)
    for n in range(blocks):
        maxima.ag[n].wait_recv()

    prefix.sent()
    maxima.sent()
    halo_sent(lpair)
    for n in range(blocks):
        halo_sent(fpairs[n])
        halo_sent(qpairs[n])


def on_device(dims, measured, estimate, extinction, psf_rows, psf_cols, stratum, seam_flags):
    depth_count, tile_count, planes, rows, cols, reach = dims
    strata, length = psf_rows.shape
    wide = rows + 2 * reach
    blocks = cols // BLOCK
    half = rows // 2
    bits = depth_count.bit_length() - 1
    steps = bits - 1
    groups = 2 if steps == 2 else 1
    collectives = 2 * (2 + steps * groups)
    f32, bf16 = jnp.float32, jnp.bfloat16
    whole = (planes, rows, cols)
    return pl.pallas_call(
        functools.partial(kernel, dims),
        out_shape=(jax.ShapeDtypeStruct(whole, f32), jax.ShapeDtypeStruct((rows, cols), f32)),
        in_specs=[
            pl.BlockSpec(memory_space=pltpu.VMEM),
            pl.BlockSpec(memory_space=pltpu.VMEM),
            pl.BlockSpec(memory_space=pltpu.SMEM),
            pl.BlockSpec(memory_space=pltpu.SMEM),
            pl.BlockSpec(memory_space=pl.ANY),
            pl.BlockSpec(memory_space=pl.ANY),
            pl.BlockSpec(memory_space=pl.ANY),
        ],
        out_specs=(pl.BlockSpec(memory_space=pltpu.VMEM), pl.BlockSpec(memory_space=pltpu.VMEM)),
        scratch_shapes=[
            pltpu.VMEM(whole, f32),
            pltpu.VMEM(whole, f32),
            pltpu.VMEM(whole, f32),
            pltpu.VMEM(whole, f32),
            pltpu.VMEM((3 * wide, BLOCK), bf16),
            pltpu.VMEM((2, strata, 4 * BLOCK), f32),
            pltpu.VMEM((2, strata, 2 * BLOCK), f32),
            pltpu.VMEM((2 * planes, rows, 4 * BLOCK), bf16),
            pltpu.VMEM((2 * planes, 2 * BLOCK, BLOCK), bf16),
            pltpu.VMEM((2 * planes, 2 * BLOCK, BLOCK), bf16),
            pltpu.VMEM((planes, rows, cols + 2 * SIDE), bf16),
            pltpu.VMEM((planes, rows, cols + 2 * SIDE), bf16),
            pltpu.VMEM((rows, cols), f32),
            pltpu.VMEM((half, cols), f32),
            pltpu.VMEM((half, cols), f32),
            pltpu.VMEM((half, cols), f32),
            pltpu.VMEM((max(steps - 1, 1), half, cols), f32),
            pltpu.VMEM((steps, half, cols), f32),
            pltpu.VMEM((rows, cols), f32),
            pltpu.VMEM((rows, cols), f32),
            pltpu.VMEM((2 + steps, half, cols), f32),
            pltpu.VMEM((steps, half, cols), f32),
            pltpu.VMEM((2, planes, reach, cols), f32),
            pltpu.VMEM((2, reach, cols), f32),
            pltpu.VMEM((2, planes, reach, cols), f32),
            pltpu.SemaphoreType.DMA((2 + blocks,)),
            pltpu.SemaphoreType.DMA((2 + 2 * blocks,)),
            pltpu.SemaphoreType.DMA((2 + 2 * blocks,)),
            pltpu.SemaphoreType.DMA((2, blocks)),
            pltpu.SemaphoreType.DMA((2, blocks)),
            pltpu.SemaphoreType.DMA((collectives, blocks)),
            pltpu.SemaphoreType.DMA((collectives, blocks)),
        ],
        compiler_params=pltpu.CompilerParams(
            collective_id=0, has_side_effects=True, vmem_limit_bytes=46 * 1024 * 1024
        ),
    )(psf_rows, psf_cols, stratum, seam_flags, measured, estimate, extinction)


def solution(mesh):
    def body(measured, estimate, extinction, psf_rows, psf_cols, stratum, seam_flags):
        planes, rows, cols = measured.shape
        dims = (mesh.shape["depth"], mesh.shape["tile"], planes, rows, cols, (psf_rows.shape[1] - 1) // 2)
        return on_device(dims, measured, estimate, extinction, psf_rows, psf_cols, stratum, seam_flags)

    return jax.shard_map(
        body,
        mesh=mesh,
        in_specs=(
            P("depth", "tile", None),
            P("depth", "tile", None),
            P("depth", "tile", None),
            P(),
            P(),
            P("depth"),
            P(),
        ),
        out_specs=(P("depth", "tile", None), P("tile", None)),
        check_vma=False,
    )
```

time: 78 us -> 70 us (0.90); the launches traced: 77 us -> 69.8 us
  other arithmetic: 3.41 us -> 0 us
  Pallas kernels: 65.4 us -> 63.4 us
  local copies, waits for them, and re-layouts: 7.45 us -> 5.68 us
    pallas_call x1, Pallas kernels: 65.4 us -> 63.4 us  [on_device(): pl.pallas_call(functools.partial(kernel, dims), out_shape=(jax.ShapeDtype...]
    reduce_sum x3 -> x0, other arithmetic: 1.72 us -> none  [the longest x2 1.63 us: choose(): taps = psf / jnp.sum(psf, axis=1, keepdims=True)]
    broadcast_in_dim x3 -> x0, local copies, waits for them, and re-layouts: 1.26 us -> none  [the longest x1 0.64 us: on_device(): jnp.pad(jnp.concatenate([third] * 3, axis=1), ((0, 0), (0, 4 * BLOCK - 3...]
    div x1 -> x0, other arithmetic: 0.79 us -> none  [choose(): taps = psf / jnp.sum(psf, axis=1, keepdims=True)]
    unnamed x4 -> x10, local copies, waits for them, and re-layouts: 5.85 us -> 5.68 us
where the time goes in v2:
time: 70 us; the launch traced here: 69.8 us
  Pallas kernels  63.4 us (91%)
  local copies, waits for them, and re-layouts  5.68 us (8%)
    pallas_call x1, Pallas kernels, on_device(): pl.pallas_call(functools.partial(kernel, dims), out_shape=(jax.ShapeDtype...  63.4 us
    unnamed x10, local copies, waits for them, and re-layouts  5.68 us

profile of v2, /device:TPU:0, one launch (start us, length us, event | category | flops | bytes accessed | tf_op | source)
XLA Modules:
  0.0 69.8 jit_solution(3956141098058059796)
XLA Ops:
  0.6 0.0 copy-start
  0.6 0.7 copy-done
  1.3 0.0 copy-start.1
  1.3 0.7 copy-done.1
  2.0 0.0 copy-start.2
  2.0 0.7 copy-done.2
  2.7 0.0 copy-start.3
  2.7 0.7 copy-done.3
  3.3 63.4 %shard_map.86 = (f32[4,256,1024]{2,1,0:T(8,128)S(1)}, f32[256,1024]{1,0:T(8,128)S(1)}) custom-call(f32[16,65]{1,0:T(8,128)S(1)} %copy-done, f32[16,65]{1,0:T(8,128)S(1)} %copy-done.1, s32[4]{0:T(128)S(1)} %copy-done.2, s32[3]{0:T(128)S(1)} %copy-done.3, f32[4,256,1024]{2,1,0:T(8,128)} %meas_hbm.1, f32[4,256,1024]{2,1,0:T(8,128)} %est_hbm.1, ...), custom_call_target="tpu_custom_call" | custom-call | tf_op jit(solution)/shard_map/pallas_call | solution.py:471
  66.8 2.0 %copy.11 = f32[4,256,1024]{2,1,0:T(8,128)} copy(f32[4,256,1024]{2,1,0:T(8,128)S(1)} %get-tuple-element.4) | data formatting | bytes 8388608
  68.8 1.0 %copy.12 = f32[256,1024]{1,0:T(8,128)} copy(f32[256,1024]{1,0:T(8,128)S(1)} %get-tuple-element.5) | data formatting | bytes 2097152
Async XLA Ops:
  0.6 0.7 %copy-start = (f32[16,65]{1,0:T(8,128)S(1)}, f32[16,65]{1,0:T(8,128)}, u32[]{:S(2)}) copy-start(f32[16,65]{1,0:T(8,128)} %psf_rows.1) | copy-start | bytes 12484
  1.3 0.7 copy-start.1
  2.0 0.7 copy-start.2
  2.7 0.7 copy-start.3

commit v3 on v2

--- a/solution.py
+++ b/solution.py
@@ -19,8 +19,8 @@
 
 
 def kernel(
-    dims, psf_rows, psf_cols, stratum, seams, meas_hbm, est_hbm, ext_hbm, upd, proj,
-    meas, est, ext, local, stacked, tall_table, flat_table, vband, lhigh, llow, mhigh, mlow,
+    dims, psf_rows_hbm, psf_cols_hbm, stratum, seams, meas_hbm, est_hbm, ext_hbm, upd, proj,
+    psf_rows, psf_cols, meas, est, ext, local, stacked, tall_table, flat_table, vband, lhigh, llow, mhigh, mlow,
     slab, pooled, carried, sums, message, landed, above, peak, mpool, mland,
     lhalo, fhalo, qhalo,
     in_sem, hal_send, hal_recv, q_send, q_recv, col_send, col_recv,
@@ -58,8 +58,12 @@
     get_ext = [loads(2 + n, ext_hbm.at[:, :, span(n)], ext.at[:, :, span(n)]) for n in range(blocks)]
     get_est = loads(0, est_hbm, est)
     get_meas = loads(1, meas_hbm, meas)
+    get_rows = loads(2 + blocks, psf_rows_hbm, psf_rows)
+    get_cols = loads(3 + blocks, psf_cols_hbm, psf_cols)
     for n in range(blocks):
         get_ext[n].start()
+    get_rows.start()
+    get_cols.start()
     get_est.start()
     get_meas.start()
 
@@ -115,7 +119,11 @@
             body(pl.ds(pl.multiple_of(i * size, size), size))
             return 0
 
-        lax.fori_loop(0, count // size, one, 0)
+        if count // size <= 4:
+            for i in range(count // size):
+                body(pl.ds(i * size, size))
+        else:
+            lax.fori_loop(0, count // size, one, 0)
 
     core = bit(0)
     own = pl.multiple_of(core * half, half)
@@ -198,6 +206,8 @@
     )
     halo_start(lpair)
 
+    get_rows.wait()
+    get_cols.wait()
     strata, length = psf_rows.shape
     highest = lax.Precision.HIGHEST
 
@@ -320,7 +330,7 @@
         def one(p, _):
             put(edge(0, p), 0, reach)
             put(edge(1, p), rows + reach, reach)
-            over(rows, lambda at: put(inner(p, at), pl.multiple_of(at.start + reach, 32), chunk))
+            over(rows, lambda at: put(inner(p, at), at.start + reach, chunk))
             mixed = jnp.dot(vband[which * planes + p, :, : 3 * wide], stacked[...], preferred_element_type=jnp.float32)
             high, low = split(mixed)
             mhigh[p, :, SIDE + n * BLOCK : SIDE + (n + 1) * BLOCK] = high
@@ -472,8 +482,8 @@
         functools.partial(kernel, dims),
         out_shape=(jax.ShapeDtypeStruct(whole, f32), jax.ShapeDtypeStruct((rows, cols), f32)),
         in_specs=[
-            pl.BlockSpec(memory_space=pltpu.VMEM),
-            pl.BlockSpec(memory_space=pltpu.VMEM),
+            pl.BlockSpec(memory_space=pltpu.HBM),
+            pl.BlockSpec(memory_space=pltpu.HBM),
             pl.BlockSpec(memory_space=pltpu.SMEM),
             pl.BlockSpec(memory_space=pltpu.SMEM),
             pl.BlockSpec(memory_space=pl.ANY),
@@ -482,6 +492,8 @@
         ],
         out_specs=(pl.BlockSpec(memory_space=pltpu.VMEM), pl.BlockSpec(memory_space=pltpu.VMEM)),
         scratch_shapes=[
+            pltpu.VMEM((strata, length), f32),
+            pltpu.VMEM((strata, length), f32),
             pltpu.VMEM(whole, f32),
             pltpu.VMEM(whole, f32),
             pltpu.VMEM(whole, f32),
@@ -507,7 +519,7 @@
             pltpu.VMEM((2, planes, reach, cols), f32),
             pltpu.VMEM((2, reach, cols), f32),
             pltpu.VMEM((2, planes, reach, cols), f32),
-            pltpu.SemaphoreType.DMA((2 + blocks,)),
+            pltpu.SemaphoreType.DMA((4 + blocks,)),
             pltpu.SemaphoreType.DMA((2 + 2 * blocks,)),
             pltpu.SemaphoreType.DMA((2 + 2 * blocks,)),
             pltpu.SemaphoreType.DMA((2, blocks)),

time: 70 us -> 68 us (0.971)
  Pallas kernels: 63.4 us -> 61.5 us
    pallas_call x1, Pallas kernels: 63.4 us -> 61.5 us  [on_device(): pl.pallas_call(functools.partial(kernel, dims), out_shape=(jax.ShapeDtype...]
where the time goes in v3:
time: 68 us; the launch traced here: 67.8 us
  Pallas kernels  61.5 us (90%)
  local copies, waits for them, and re-layouts  5.68 us (8%)
    pallas_call x1, Pallas kernels, on_device(): pl.pallas_call(functools.partial(kernel, dims), out_shape=(jax.ShapeDtype...  61.5 us
    unnamed x10, local copies, waits for them, and re-layouts  5.68 us

profile of v3, /device:TPU:0, one launch (start us, length us, event | category | flops | bytes accessed | tf_op | source)
XLA Modules:
  0.0 67.8 jit_solution(11551083451921529094)
XLA Ops:
  0.6 0.0 copy-start
  0.6 0.7 %copy-done = f32[16,65]{1,0:T(8,128)S(1)} copy-done((f32[16,65]{1,0:T(8,128)S(1)}, f32[16,65]{1,0:T(8,128)}, u32[]{:S(2)}) %copy-start) | copy-done | bytes 4184
  1.3 0.0 copy-start.1
  1.3 0.7 %copy-done.1 = f32[16,65]{1,0:T(8,128)S(1)} copy-done((f32[16,65]{1,0:T(8,128)S(1)}, f32[16,65]{1,0:T(8,128)}, u32[]{:S(2)}) %copy-start.1) | copy-done | bytes 4184
  2.0 0.0 copy-start.2
  2.0 0.7 copy-done.2
  2.7 0.0 copy-start.3
  2.7 0.7 copy-done.3
  3.3 61.5 %shard_map.86 = (f32[4,256,1024]{2,1,0:T(8,128)S(1)}, f32[256,1024]{1,0:T(8,128)S(1)}) custom-call(f32[16,65]{1,0:T(8,128)S(1)} %copy-done, f32[16,65]{1,0:T(8,128)S(1)} %copy-done.1, s32[4]{0:T(128)S(1)} %copy-done.2, s32[3]{0:T(128)S(1)} %copy-done.3, f32[4,256,1024]{2,1,0:T(8,128)} %meas_hbm.1, f32[4,256,1024]{2,1,0:T(8,128)} %est_hbm.1, ...), custom_call_target="tpu_custom_call" | custom-call | tf_op jit(solution)/shard_map/pallas_call | solution.py:481
  64.8 2.0 %copy.11 = f32[4,256,1024]{2,1,0:T(8,128)} copy(f32[4,256,1024]{2,1,0:T(8,128)S(1)} %get-tuple-element.4) | data formatting | bytes 8388608
  66.8 1.0 %copy.12 = f32[256,1024]{1,0:T(8,128)} copy(f32[256,1024]{1,0:T(8,128)S(1)} %get-tuple-element.5) | data formatting | bytes 2097152
Async XLA Ops:
  0.6 0.7 %copy-start = (f32[16,65]{1,0:T(8,128)S(1)}, f32[16,65]{1,0:T(8,128)}, u32[]{:S(2)}) copy-start(f32[16,65]{1,0:T(8,128)} %psf_rows_hbm.1) | copy-start | bytes 12484
  1.3 0.7 %copy-start.1 = (f32[16,65]{1,0:T(8,128)S(1)}, f32[16,65]{1,0:T(8,128)}, u32[]{:S(2)}) copy-start(f32[16,65]{1,0:T(8,128)} %psf_cols_hbm.1) | copy-start | bytes 12484
  2.0 0.7 copy-start.2
  2.7 0.7 copy-start.3
